TPU v7x, 32 devices: a whole 2x2x4 slice. The times are simulated.
32 devices in a mesh: group: 2 (over y), src: 4 (over z), rcv: 4 (over x, core).
Axes of the slice: x: 2, y: 2, z: 4, core: 2. Of those that a mesh axis runs over, the one named last changes fastest.
Arguments:
- traces: bfloat16 [128, 36864], P(('group', 'src', 'rcv')), parts along dimension 0, may hold values from -6 to 6
- offsets: int32 [16], P('group'), parts along dimension 0, may hold values from 0 to 32768
- receiver_slots: int32 [8, 16], P(('group', 'rcv')), parts along dimension 0, may hold values from 0 to 15, each once within a row
Outputs:
- correlations: bfloat16 [128, 64, 128], P(('group', 'src'), 'rcv'), parts along dimension 0
There are 2 independent parts, one for each index of `group`. A program takes and returns all parts, laid end to end along the dimension named above; each array names one. Nothing has to cross between parts.
All inputs are finite; a program needn't handle non-finite values.
Results may differ from a plain program's by a relative error of at most 0.0065.
Values may be sent and summed in bfloat16 or wider, within the bound.
No kernel may reach another device: no remote copies, remote signals or barrier semaphores. Data moves between devices by JAX's collectives and lax.ppermute only.
A program may use at most 64 MiB of HBM per device.

v0:
```python
import math
import jax
import jax.numpy as jnp
from jax import lax
from jax.sharding import PartitionSpec as P

SEG_LEN = 4096
NB = 512
LAGS = 128
LAG_STEP = 4
SEGS = 8


def dft_table():
    t_index = jnp.arange(SEG_LEN, dtype=jnp.int32)[:, None]
    k_index = jnp.arange(NB, dtype=jnp.int32)[None, :]
    phase = jnp.mod(t_index * k_index, SEG_LEN).astype(jnp.float32) * (2.0 * math.pi / SEG_LEN)
    return jnp.concatenate([jnp.cos(phase), -jnp.sin(phase)], axis=1).astype(jnp.bfloat16)


def lag_table():
    k_index = jnp.arange(NB, dtype=jnp.int32)[:, None]
    lag_shift = LAG_STEP * (jnp.arange(LAGS, dtype=jnp.int32)[None, :] - LAGS // 2)
    phase = jnp.mod(k_index * lag_shift, SEG_LEN).astype(jnp.float32) * (2.0 * math.pi / SEG_LEN)
    return jnp.concatenate([jnp.cos(phase), -jnp.sin(phase)], axis=0).astype(jnp.bfloat16)


def whiten(traces, offsets):
    table = dft_table()
    pieces = jax.vmap(lambda start: lax.dynamic_slice_in_dim(traces, start, SEG_LEN, 1))(offsets)
    pieces = jnp.transpose(pieces, (1, 0, 2)).reshape(-1, SEG_LEN)
    spectra = jnp.dot(pieces, table, preferred_element_type=jnp.float32)
    energy = jnp.mean(spectra * spectra, axis=-1, keepdims=True)
    white = (spectra / jnp.sqrt(energy + 1e-06)).astype(jnp.bfloat16)
    return white.reshape(traces.shape[0], SEGS, 2 * NB)


def four_sources(sources, receivers, lags):
    src_re = sources[..., :NB]
    src_im = sources[..., NB:]
    rec_re = receivers[..., :NB]
    rec_im = receivers[..., NB:]

    def pair(left, right):
        return jnp.einsum("sgk,rgk->srk", left, right, preferred_element_type=jnp.float32)

    real_part = pair(src_re, rec_re) + pair(src_im, rec_im)
    imag_part = pair(src_re, rec_im) - pair(src_im, rec_re)
    cross = jnp.concatenate([real_part, imag_part], axis=-1).astype(jnp.bfloat16)
    out = jnp.einsum("srk,kl->srl", cross, lags, preferred_element_type=jnp.float32)
    return (out * (1.0 / math.sqrt(SEGS * NB))).astype(jnp.bfloat16)


def correlate(sources, receivers, lags):
    src_count = sources.shape[0]
    grouped = sources.reshape(src_count // 4, 4, SEGS, 2 * NB)
    out = lax.map(lambda blk: four_sources(blk, receivers, lags), grouped)
    return out.reshape(src_count, receivers.shape[0], LAGS)


def on_device(traces, offsets, receiver_slots):
    white = whiten(traces, offsets)
    lags = lag_table()
    sources = lax.all_gather(white, "rcv", axis=0, tiled=True)
    block = correlate(sources, lax.all_gather(white, "src", axis=0, tiled=True), lags)
    return jnp.take(block, receiver_slots[0], axis=1)


def solution(mesh):
    in_specs = (P(("group", "src", "rcv"), None), P("group"), P(("group", "rcv"), None))
    out_specs = P(("group", "src"), "rcv", None)
    return jax.shard_map(
        on_device, mesh=mesh, in_specs=in_specs, out_specs=out_specs, check_vma=False
    )
```

profile of v0, /device:TPU:0, one launch (start us, length us, event | category | flops | bytes accessed | tf_op | source)
XLA Modules:
  0.0 121.1 jit_solution(13736536514290017647)
XLA Ops:
  0.0 0.7 fusion.40
  0.7 16.2 %while.12 = (s32[]{:T(128)}, bf16[4,36864]{1,0:T(4,128)(2,1)}, s32[8,2]{0,1:T(2,128)S(1)}, bf16[8,4,4096]{2,1,0:T(4,128)(2,1)S(1)}, s32[]{:T(128)}) while((s32[]{:T(128)}, bf16[4,36864]{1,0:T(4,128)(2,1)}, s32[8,2]{0,1:T(2,128)S(1)}, bf16[8,4,4096]{2,1,0:T(4,128)(2,1)S(1)}, s32[]{:T(128)}) %tuple.34), condition=%wide.while_cond, body=%wide.while_body.sunk | while | flops 2 | bytes 65633 | solution.py:30
  1.3 1.4 %bitcast_dynamic-update-slice_fusion.2 = bf16[8,4,4096]{2,1,0:T(4,128)(2,1)S(1)} fusion(bf16[8,4,4096]{2,1,0:T(4,128)(2,1)S(1)} %get-tuple-element.139, s32[]{:T(128)} %get-tuple-element.136, bf16[4,36864]{1,0:T(4,128)(2,1)} %get-tuple-element.142, s32[]{:T(128)} %bitcast.79), kind=kLoop, calls=%fused_computation.27.clone.1 | loop fusion | bytes 65544 | tf_op jit(solution)/shard_map/vmap()/gather
  3.3 1.4 %bitcast_dynamic-update-slice_fusion.2 = bf16[8,4,4096]{2,1,0:T(4,128)(2,1)S(1)} fusion(bf16[8,4,4096]{2,1,0:T(4,128)(2,1)S(1)} %get-tuple-element.139, s32[]{:T(128)} %get-tuple-element.136, bf16[4,36864]{1,0:T(4,128)(2,1)} %get-tuple-element.142, s32[]{:T(128)} %bitcast.79), kind=kLoop, calls=%fused_computation.27.clone.1 | loop fusion | bytes 65544 | tf_op jit(solution)/shard_map/vmap()/gather
  5.3 1.4 %bitcast_dynamic-update-slice_fusion.2 = bf16[8,4,4096]{2,1,0:T(4,128)(2,1)S(1)} fusion(bf16[8,4,4096]{2,1,0:T(4,128)(2,1)S(1)} %get-tuple-element.139, s32[]{:T(128)} %get-tuple-element.136, bf16[4,36864]{1,0:T(4,128)(2,1)} %get-tuple-element.142, s32[]{:T(128)} %bitcast.79), kind=kLoop, calls=%fused_computation.27.clone.1 | loop fusion | bytes 65544 | tf_op jit(solution)/shard_map/vmap()/gather
  7.3 1.4 %bitcast_dynamic-update-slice_fusion.2 = bf16[8,4,4096]{2,1,0:T(4,128)(2,1)S(1)} fusion(bf16[8,4,4096]{2,1,0:T(4,128)(2,1)S(1)} %get-tuple-element.139, s32[]{:T(128)} %get-tuple-element.136, bf16[4,36864]{1,0:T(4,128)(2,1)} %get-tuple-element.142, s32[]{:T(128)} %bitcast.79), kind=kLoop, calls=%fused_computation.27.clone.1 | loop fusion | bytes 65544 | tf_op jit(solution)/shard_map/vmap()/gather
  9.3 1.4 %bitcast_dynamic-update-slice_fusion.2 = bf16[8,4,4096]{2,1,0:T(4,128)(2,1)S(1)} fusion(bf16[8,4,4096]{2,1,0:T(4,128)(2,1)S(1)} %get-tuple-element.139, s32[]{:T(128)} %get-tuple-element.136, bf16[4,36864]{1,0:T(4,128)(2,1)} %get-tuple-element.142, s32[]{:T(128)} %bitcast.79), kind=kLoop, calls=%fused_computation.27.clone.1 | loop fusion | bytes 65544 | tf_op jit(solution)/shard_map/vmap()/gather
  11.4 1.4 %bitcast_dynamic-update-slice_fusion.2 = bf16[8,4,4096]{2,1,0:T(4,128)(2,1)S(1)} fusion(bf16[8,4,4096]{2,1,0:T(4,128)(2,1)S(1)} %get-tuple-element.139, s32[]{:T(128)} %get-tuple-element.136, bf16[4,36864]{1,0:T(4,128)(2,1)} %get-tuple-element.142, s32[]{:T(128)} %bitcast.79), kind=kLoop, calls=%fused_computation.27.clone.1 | loop fusion | bytes 65544 | tf_op jit(solution)/shard_map/vmap()/gather
  13.4 1.4 %bitcast_dynamic-update-slice_fusion.2 = bf16[8,4,4096]{2,1,0:T(4,128)(2,1)S(1)} fusion(bf16[8,4,4096]{2,1,0:T(4,128)(2,1)S(1)} %get-tuple-element.139, s32[]{:T(128)} %get-tuple-element.136, bf16[4,36864]{1,0:T(4,128)(2,1)} %get-tuple-element.142, s32[]{:T(128)} %bitcast.79), kind=kLoop, calls=%fused_computation.27.clone.1 | loop fusion | bytes 65544 | tf_op jit(solution)/shard_map/vmap()/gather
  15.4 1.4 %bitcast_dynamic-update-slice_fusion.2 = bf16[8,4,4096]{2,1,0:T(4,128)(2,1)S(1)} fusion(bf16[8,4,4096]{2,1,0:T(4,128)(2,1)S(1)} %get-tuple-element.139, s32[]{:T(128)} %get-tuple-element.136, bf16[4,36864]{1,0:T(4,128)(2,1)} %get-tuple-element.142, s32[]{:T(128)} %bitcast.79), kind=kLoop, calls=%fused_computation.27.clone.1 | loop fusion | bytes 65544 | tf_op jit(solution)/shard_map/vmap()/gather
  16.8 33.9 %negate_convert_fusion = (bf16[4096,512]{1,0:T(8,128)(2,1)S(1)}, bf16[4096,512]{1,0:T(8,128)(2,1)S(1)}) fusion(), kind=kLoop, calls=%fused_computation.39 | loop fusion | flops 35651584 | bytes 8388608 | tf_op jit(solution)/shard_map/convert.7
  50.8 1.6 %multiply_reduce_fusion = (f32[32]{0:T(128)S(1)}, f32[32,1024]{1,0:T(8,128)S(1)}) fusion(bf16[4096,512]{1,0:T(8,128)(2,1)S(1)} %get-tuple-element.73, bf16[4096,512]{1,0:T(8,128)(2,1)S(1)} %get-tuple-element.74, bf16[8,4,4096]{2,1,0:T(4,128)(2,1)S(1)} %get-tuple-element.40), kind=kOutput, calls=%fused_computation.59 | convolution fusion | flops 285278176 | bytes 8781952 | tf_op jit(solution)/shard_map/dot_general | solution.py:32
  52.5 15.7 %all_gather.7 = bf16[16,8,1024]{2,1,0:T(8,128)(2,1)S(1)} all-gather(bf16[4,8,1024]{2,1,0:T(8,128)(2,1)S(1)} %fusion.39), channel_id=1, replica_groups=mesh['group'=2,'src'=4,'rcv'=4] {'src'}, dimensions={0}, use_global_device_ids=true | all-gather | bytes 327680 | tf_op jit(solution)/shard_map/all_gather | solution.py:65
  68.2 1.6 %copy.17 = bf16[16,8,1024]{0,1,2:T(8,128)(2,1)S(1)} copy(bf16[16,8,1024]{2,1,0:T(8,128)(2,1)S(1)} %all_gather.7) | data formatting | bytes 524288 | tf_op jit(solution)/shard_map/while | solution.py:57
  69.8 6.2 %all_gather.6 = bf16[16,8,1024]{2,1,0:T(8,128)(2,1)} all-gather(bf16[4,8,1024]{2,1,0:T(8,128)(2,1)S(1)} %fusion.39), channel_id=1, replica_groups=mesh['group'=2,'src'=4,'rcv'=4] {'rcv'}, dimensions={0}, use_global_device_ids=true | all-gather | bytes 327680 | tf_op jit(solution)/shard_map/all_gather | solution.py:64
  76.1 1.1 cosine_convert_fusion.1
  77.2 0.7 pad_maximum_fusion
  77.9 41.0 %while.11 = (s32[]{:T(128)}, bf16[4,4,16,128]{3,1,0,2:T(4,128)(2,1)}, bf16[4,4,8,1024]{3,2,1,0:T(8,128)(2,1)}, bf16[16,8,1024]{0,1,2:T(8,128)(2,1)S(1)}, bf16[1024,128]{1,0:T(8,128)(2,1)}, /*index=5*/s32[]{:T(128)}) while((s32[]{:T(128)}, bf16[4,4,16,128]{3,1,0,2:T(4,128)(2,1)}, bf16[4,4,8,1024]{3,2,1,0:T(8,128)(2,1)}, ...), condition=%wide.region_2.3_spmd, body=%wide.region_1.2_spmd.sunk | while | flops 19283968 | bytes 4768385 | solution.py:57
  77.9 0.9 constant_dynamic-slice_fusion.4
  78.8 0.7 copy.35
  79.5 0.7 fusion.97
  80.3 1.5 %fusion.99 = bf16[4,16,512]{1,0,2:T(4,128)(2,1)} fusion(f32[512,4,16]{2,1,0:T(4,128)S(1)} %fusion.97, bf16[1,4,8,1024]{2,1,3,0:T(4,128)(2,1)S(1)} %copy.35, bf16[16,8,512]{0,1,2:T(8,128)(2,1)S(1)} %fusion.98), kind=kOutput, calls=%fused_computation.6.clone.2 | convolution fusion | flops 589824 | bytes 393216 | tf_op jit(solution)/shard_map/while/body/eval_jaxpr/sgk,rgk->srk/dot_general | solution.py:45
  81.8 1.9 %copy.37 = bf16[4,16,512]{2,1,0:T(8,128)(2,1)} copy(bf16[4,16,512]{1,0,2:T(4,128)(2,1)} %fusion.99) | data formatting | bytes 131072 | tf_op jit(solution)/shard_map/while/body/eval_jaxpr/add | solution.py:47
  83.8 0.7 fusion.93
  84.6 1.5 %fusion.95 = bf16[4,16,512]{1,0,2:T(4,128)(2,1)} fusion(f32[512,4,16]{2,1,0:T(4,128)S(1)} %fusion.93, bf16[1,4,8,1024]{2,1,3,0:T(4,128)(2,1)S(1)} %copy.35, bf16[16,8,512]{0,1,2:T(8,128)(2,1)S(1)} %fusion.94), kind=kOutput, calls=%fused_computation.5.clone.2 | convolution fusion | flops 589824 | bytes 393216 | tf_op jit(solution)/shard_map/while/body/eval_jaxpr/sgk,rgk->srk/dot_general | solution.py:45
  86.1 1.3 %copy.36 = bf16[4,16,512]{2,1,0:T(8,128)(2,1)S(1)} copy(bf16[4,16,512]{1,0,2:T(4,128)(2,1)} %fusion.95) | data formatting | bytes 131072 | tf_op jit(solution)/shard_map/while/body/eval_jaxpr/sub | solution.py:48
  88.2 0.8 constant_dynamic-slice_fusion.4
  89.8 0.7 fusion.97
  90.5 1.5 %fusion.99 = bf16[4,16,512]{1,0,2:T(4,128)(2,1)} fusion(f32[512,4,16]{2,1,0:T(4,128)S(1)} %fusion.97, bf16[1,4,8,1024]{2,1,3,0:T(4,128)(2,1)S(1)} %copy.35, bf16[16,8,512]{0,1,2:T(8,128)(2,1)S(1)} %fusion.98), kind=kOutput, calls=%fused_computation.6.clone.2 | convolution fusion | flops 589824 | bytes 393216 | tf_op jit(solution)/shard_map/while/body/eval_jaxpr/sgk,rgk->srk/dot_general | solution.py:45
  92.1 1.9 %copy.37 = bf16[4,16,512]{2,1,0:T(8,128)(2,1)} copy(bf16[4,16,512]{1,0,2:T(4,128)(2,1)} %fusion.99) | data formatting | bytes 131072 | tf_op jit(solution)/shard_map/while/body/eval_jaxpr/add | solution.py:47
  94.0 0.7 fusion.93
  94.8 1.5 %fusion.95 = bf16[4,16,512]{1,0,2:T(4,128)(2,1)} fusion(f32[512,4,16]{2,1,0:T(4,128)S(1)} %fusion.93, bf16[1,4,8,1024]{2,1,3,0:T(4,128)(2,1)S(1)} %copy.35, bf16[16,8,512]{0,1,2:T(8,128)(2,1)S(1)} %fusion.94), kind=kOutput, calls=%fused_computation.5.clone.2 | convolution fusion | flops 589824 | bytes 393216 | tf_op jit(solution)/shard_map/while/body/eval_jaxpr/sgk,rgk->srk/dot_general | solution.py:45
  96.4 1.3 %copy.36 = bf16[4,16,512]{2,1,0:T(8,128)(2,1)S(1)} copy(bf16[4,16,512]{1,0,2:T(4,128)(2,1)} %fusion.95) | data formatting | bytes 131072 | tf_op jit(solution)/shard_map/while/body/eval_jaxpr/sub | solution.py:48
  98.4 0.8 constant_dynamic-slice_fusion.4
  100.0 0.7 fusion.97
  100.8 1.5 %fusion.99 = bf16[4,16,512]{1,0,2:T(4,128)(2,1)} fusion(f32[512,4,16]{2,1,0:T(4,128)S(1)} %fusion.97, bf16[1,4,8,1024]{2,1,3,0:T(4,128)(2,1)S(1)} %copy.35, bf16[16,8,512]{0,1,2:T(8,128)(2,1)S(1)} %fusion.98), kind=kOutput, calls=%fused_computation.6.clone.2 | convolution fusion | flops 589824 | bytes 393216 | tf_op jit(solution)/shard_map/while/body/eval_jaxpr/sgk,rgk->srk/dot_general | solution.py:45
  102.3 1.9 %copy.37 = bf16[4,16,512]{2,1,0:T(8,128)(2,1)} copy(bf16[4,16,512]{1,0,2:T(4,128)(2,1)} %fusion.99) | data formatting | bytes 131072 | tf_op jit(solution)/shard_map/while/body/eval_jaxpr/add | solution.py:47
  104.3 0.7 fusion.93
  105.1 1.5 %fusion.95 = bf16[4,16,512]{1,0,2:T(4,128)(2,1)} fusion(f32[512,4,16]{2,1,0:T(4,128)S(1)} %fusion.93, bf16[1,4,8,1024]{2,1,3,0:T(4,128)(2,1)S(1)} %copy.35, bf16[16,8,512]{0,1,2:T(8,128)(2,1)S(1)} %fusion.94), kind=kOutput, calls=%fused_computation.5.clone.2 | convolution fusion | flops 589824 | bytes 393216 | tf_op jit(solution)/shard_map/while/body/eval_jaxpr/sgk,rgk->srk/dot_general | solution.py:45
  106.6 1.3 %copy.36 = bf16[4,16,512]{2,1,0:T(8,128)(2,1)S(1)} copy(bf16[4,16,512]{1,0,2:T(4,128)(2,1)} %fusion.95) | data formatting | bytes 131072 | tf_op jit(solution)/shard_map/while/body/eval_jaxpr/sub | solution.py:48
  108.7 0.8 constant_dynamic-slice_fusion.4
  110.3 0.7 fusion.97
  111.0 1.5 %fusion.99 = bf16[4,16,512]{1,0,2:T(4,128)(2,1)} fusion(f32[512,4,16]{2,1,0:T(4,128)S(1)} %fusion.97, bf16[1,4,8,1024]{2,1,3,0:T(4,128)(2,1)S(1)} %copy.35, bf16[16,8,512]{0,1,2:T(8,128)(2,1)S(1)} %fusion.98), kind=kOutput, calls=%fused_computation.6.clone.2 | convolution fusion | flops 589824 | bytes 393216 | tf_op jit(solution)/shard_map/while/body/eval_jaxpr/sgk,rgk->srk/dot_general | solution.py:45
  112.6 1.9 %copy.37 = bf16[4,16,512]{2,1,0:T(8,128)(2,1)} copy(bf16[4,16,512]{1,0,2:T(4,128)(2,1)} %fusion.99) | data formatting | bytes 131072 | tf_op jit(solution)/shard_map/while/body/eval_jaxpr/add | solution.py:47
  114.6 0.7 fusion.93
  115.3 1.5 %fusion.95 = bf16[4,16,512]{1,0,2:T(4,128)(2,1)} fusion(f32[512,4,16]{2,1,0:T(4,128)S(1)} %fusion.93, bf16[1,4,8,1024]{2,1,3,0:T(4,128)(2,1)S(1)} %copy.35, bf16[16,8,512]{0,1,2:T(8,128)(2,1)S(1)} %fusion.94), kind=kOutput, calls=%fused_computation.5.clone.2 | convolution fusion | flops 589824 | bytes 393216 | tf_op jit(solution)/shard_map/while/body/eval_jaxpr/sgk,rgk->srk/dot_general | solution.py:45
  116.9 1.3 %copy.36 = bf16[4,16,512]{2,1,0:T(8,128)(2,1)S(1)} copy(bf16[4,16,512]{1,0,2:T(4,128)(2,1)} %fusion.95) | data formatting | bytes 131072 | tf_op jit(solution)/shard_map/while/body/eval_jaxpr/sub | solution.py:48
  119.0 1.4 %gather_fusion = bf16[16,16,128]{2,1,0:T(8,128)(2,1)S(1)} fusion(bf16[16,16,128]{2,0,1:T(8,128)(2,1)} %bitcast.80, s32[1024]{0:T(1024)S(1)} %pad_clamp_fusion), kind=kCustom, calls=%fused_computation | custom fusion | bytes 131136 | tf_op jit(solution)/shard_map/jit(_take)/gather | solution.py:66
  (72 shorter events, 11.9 us)
Async XLA Ops:
  77.9 41.0 %copy-start.2 = (s32[1,16]{1,0:T(1,128)S(1)}, s32[1,16]{1,0:T(1,128)}, u32[]{:S(2)}) copy-start(s32[1,16]{1,0:T(1,128)} %param.7) | copy-start | bytes 196
  84.5 2.8 %copy-start = (bf16[1024,128]{1,0:T(8,128)(2,1)S(1)}, bf16[1024,128]{1,0:T(8,128)(2,1)}, u32[]{:S(2)}) copy-start(bf16[1024,128]{1,0:T(8,128)(2,1)} %get-tuple-element.162) | copy-start | bytes 786436 | tf_op jit(solution)/shard_map/while
  84.6 2.8 %copy-start.1 = (bf16[4,16,512]{2,1,0:T(8,128)(2,1)S(1)}, bf16[4,16,512]{2,1,0:T(8,128)(2,1)}, u32[]{:S(2)}) copy-start(bf16[4,16,512]{2,1,0:T(8,128)(2,1)} %copy.37) | copy-start | bytes 196612 | tf_op jit(solution)/shard_map/while
  94.8 2.8 %copy-start = (bf16[1024,128]{1,0:T(8,128)(2,1)S(1)}, bf16[1024,128]{1,0:T(8,128)(2,1)}, u32[]{:S(2)}) copy-start(bf16[1024,128]{1,0:T(8,128)(2,1)} %get-tuple-element.162) | copy-start | bytes 786436 | tf_op jit(solution)/shard_map/while
  94.8 2.8 %copy-start.1 = (bf16[4,16,512]{2,1,0:T(8,128)(2,1)S(1)}, bf16[4,16,512]{2,1,0:T(8,128)(2,1)}, u32[]{:S(2)}) copy-start(bf16[4,16,512]{2,1,0:T(8,128)(2,1)} %copy.37) | copy-start | bytes 196612 | tf_op jit(solution)/shard_map/while
  105.1 2.8 %copy-start = (bf16[1024,128]{1,0:T(8,128)(2,1)S(1)}, bf16[1024,128]{1,0:T(8,128)(2,1)}, u32[]{:S(2)}) copy-start(bf16[1024,128]{1,0:T(8,128)(2,1)} %get-tuple-element.162) | copy-start | bytes 786436 | tf_op jit(solution)/shard_map/while
  105.1 2.8 %copy-start.1 = (bf16[4,16,512]{2,1,0:T(8,128)(2,1)S(1)}, bf16[4,16,512]{2,1,0:T(8,128)(2,1)}, u32[]{:S(2)}) copy-start(bf16[4,16,512]{2,1,0:T(8,128)(2,1)} %copy.37) | copy-start | bytes 196612 | tf_op jit(solution)/shard_map/while
  115.3 2.8 %copy-start = (bf16[1024,128]{1,0:T(8,128)(2,1)S(1)}, bf16[1024,128]{1,0:T(8,128)(2,1)}, u32[]{:S(2)}) copy-start(bf16[1024,128]{1,0:T(8,128)(2,1)} %get-tuple-element.162) | copy-start | bytes 786436 | tf_op jit(solution)/shard_map/while
  115.3 2.8 %copy-start.1 = (bf16[4,16,512]{2,1,0:T(8,128)(2,1)S(1)}, bf16[4,16,512]{2,1,0:T(8,128)(2,1)}, u32[]{:S(2)}) copy-start(bf16[4,16,512]{2,1,0:T(8,128)(2,1)} %copy.37) | copy-start | bytes 196612 | tf_op jit(solution)/shard_map/while
where the time goes:
time: 122 us; the launch traced here: 121 us
  local copies, waits for them, and re-layouts  42.1 us (35%)
  other arithmetic  36.6 us (30%)
  blocking collectives  21.9 us (18%)
  matrix products  20 us (16%)
    another operation x2, other arithmetic  35 us
    dot_general x16, matrix products, pair(): jnp.einsum('sgk,rgk->srk', left, right, preferred_element_type=jnp.float32)  17.6 us
    gather x24, local copies, waits for them, and re-layouts  16 us
    all_gather x1, blocking collectives, on_device(): lax.all_gather(white, 'src', axis=0, tiled=True)  15.7 us
    add x4, local copies, waits for them, and re-layouts, four_sources(): real_part = pair(src_re, rec_re) + pair(src_im, rec_im)  7.62 us
    all_gather x1, blocking collectives, on_device(): sources = lax.all_gather(white, 'rcv', axis=0, tiled=True)  6.23 us
    dynamic_slice x8, local copies, waits for them, and re-layouts, correlate(): out = lax.map(lambda blk: four_sources(blk, receivers, lags), grouped)  6.01 us
    sub x4, local copies, waits for them, and re-layouts, four_sources(): imag_part = pair(src_re, rec_im) - pair(src_im, rec_re)  5.05 us

commit v1 on v0

--- a/solution.py
+++ b/solution.py
@@ -61,7 +61,13 @@
 def on_device(traces, offsets, receiver_slots):
     white = whiten(traces, offsets)
     lags = lag_table()
-    sources = lax.all_gather(white, "rcv", axis=0, tiled=True)
+    count = lax.axis_size("rcv")
+    held, blocks = (white, [white])
+    for _ in range(count - 1):
+        held = lax.ppermute(held, "rcv", [(i, (i + 1) % count) for i in range(count)])
+        blocks.insert(0, held)
+    flat = jnp.concatenate(blocks, axis=0)
+    sources = jnp.roll(flat, (lax.axis_index("rcv") + 1) * white.shape[0], axis=0)
     block = correlate(sources, lax.all_gather(white, "src", axis=0, tiled=True), lags)
     return jnp.take(block, receiver_slots[0], axis=1)
 

time: 122 us -> 129 us (1.057)
  blocking collectives: 21.9 us -> 15.7 us
  waiting for transfers between devices: 0 us -> 6.06 us
  matrix products: 20 us -> 22.8 us
  other arithmetic: 36.6 us -> 38.4 us
    all_gather x1 -> x0, blocking collectives: 6.23 us -> none  [on_device(): sources = lax.all_gather(white, 'rcv', axis=0, tiled=True)]
    ppermute x0 -> x3, waiting for transfers between devices: none -> 6.06 us  [on_device(): lax.ppermute(held, 'rcv', [(i, (i + 1) % count) for i in range(count)])]
    dot_general x1, matrix products: 1.63 us -> 4.42 us  [whiten(): spectra = jnp.dot(pieces, table, preferred_element_type=jnp.float32)]
  transfers between devices with their start and end apart: 0 -> 3, of which waited for: 0 -> 2; matrix products, arithmetic and copies ran while one was open for 0% -> 4% of each run, Pallas kernels for 0% -> 0%
where the time goes in v1:
time: 129 us; the launch traced here: 127 us
  local copies, waits for them, and re-layouts  43.2 us (33%)
  other arithmetic  38.4 us (30%)
  matrix products  22.8 us (18%)
  blocking collectives  15.7 us (12%)
  waiting for transfers between devices  6.06 us (5%)
    another operation x2, other arithmetic  36.2 us
    dot_general x16, matrix products, pair(): jnp.einsum('sgk,rgk->srk', left, right, preferred_element_type=jnp.float32)  17.7 us
    gather x24, local copies, waits for them, and re-layouts  16.2 us
    all_gather x1, blocking collectives, on_device(): lax.all_gather(white, 'src', axis=0, tiled=True)  15.7 us
    add x4, local copies, waits for them, and re-layouts, four_sources(): real_part = pair(src_re, rec_re) + pair(src_im, rec_im)  7.67 us
    ppermute x3, waiting for transfers between devices, on_device(): lax.ppermute(held, 'rcv', [(i, (i + 1) % count) for i in range(count)])  6.06 us
    dynamic_slice x8, local copies, waits for them, and re-layouts, correlate(): out = lax.map(lambda blk: four_sources(blk, receivers, lags), grouped)  6 us
    sub x4, local copies, waits for them, and re-layouts, four_sources(): imag_part = pair(src_re, rec_im) - pair(src_im, rec_re)  5.05 us
  transfers between devices with their start and end apart: 3, of which 2 were waited for; matrix products, arithmetic and copies ran while one was open for 4% of the time, Pallas kernels for 0%

profile of v1, /device:TPU:0, one launch (start us, length us, event | category | flops | bytes accessed | tf_op | source)
XLA Modules:
  0.0 127.5 jit_solution(2804812540017730210)
XLA Ops:
  0.0 35.1 %negate_convert_fusion = (bf16[4096,512]{1,0:T(8,128)(2,1)}, bf16[4096,512]{1,0:T(8,128)(2,1)}) fusion(), kind=kLoop, calls=%fused_computation.39 | loop fusion | flops 35651584 | bytes 8388608 | tf_op jit(solution)/shard_map/convert.7
  35.2 16.3 %while.12 = (s32[]{:T(128)}, bf16[4,36864]{1,0:T(4,128)(2,1)}, s32[8,2]{0,1:T(2,128)S(1)}, bf16[8,4,4096]{2,1,0:T(4,128)(2,1)S(1)}, s32[]{:T(128)}) while((s32[]{:T(128)}, bf16[4,36864]{1,0:T(4,128)(2,1)}, s32[8,2]{0,1:T(2,128)S(1)}, bf16[8,4,4096]{2,1,0:T(4,128)(2,1)S(1)}, s32[]{:T(128)}) %tuple.35), condition=%wide.while_cond, body=%wide.while_body.sunk | while | flops 2 | bytes 65633 | solution.py:30
  35.8 1.4 %bitcast_dynamic-update-slice_fusion.2 = bf16[8,4,4096]{2,1,0:T(4,128)(2,1)S(1)} fusion(bf16[8,4,4096]{2,1,0:T(4,128)(2,1)S(1)} %get-tuple-element.144, s32[]{:T(128)} %get-tuple-element.141, bf16[4,36864]{1,0:T(4,128)(2,1)} %get-tuple-element.147, s32[]{:T(128)} %bitcast.83), kind=kLoop, calls=%fused_computation.27.clone.1 | loop fusion | bytes 65544 | tf_op jit(solution)/shard_map/vmap()/gather
  37.8 1.4 %bitcast_dynamic-update-slice_fusion.2 = bf16[8,4,4096]{2,1,0:T(4,128)(2,1)S(1)} fusion(bf16[8,4,4096]{2,1,0:T(4,128)(2,1)S(1)} %get-tuple-element.144, s32[]{:T(128)} %get-tuple-element.141, bf16[4,36864]{1,0:T(4,128)(2,1)} %get-tuple-element.147, s32[]{:T(128)} %bitcast.83), kind=kLoop, calls=%fused_computation.27.clone.1 | loop fusion | bytes 65544 | tf_op jit(solution)/shard_map/vmap()/gather
  39.8 1.4 %bitcast_dynamic-update-slice_fusion.2 = bf16[8,4,4096]{2,1,0:T(4,128)(2,1)S(1)} fusion(bf16[8,4,4096]{2,1,0:T(4,128)(2,1)S(1)} %get-tuple-element.144, s32[]{:T(128)} %get-tuple-element.141, bf16[4,36864]{1,0:T(4,128)(2,1)} %get-tuple-element.147, s32[]{:T(128)} %bitcast.83), kind=kLoop, calls=%fused_computation.27.clone.1 | loop fusion | bytes 65544 | tf_op jit(solution)/shard_map/vmap()/gather
  41.9 1.4 %bitcast_dynamic-update-slice_fusion.2 = bf16[8,4,4096]{2,1,0:T(4,128)(2,1)S(1)} fusion(bf16[8,4,4096]{2,1,0:T(4,128)(2,1)S(1)} %get-tuple-element.144, s32[]{:T(128)} %get-tuple-element.141, bf16[4,36864]{1,0:T(4,128)(2,1)} %get-tuple-element.147, s32[]{:T(128)} %bitcast.83), kind=kLoop, calls=%fused_computation.27.clone.1 | loop fusion | bytes 65544 | tf_op jit(solution)/shard_map/vmap()/gather
  43.9 1.4 %bitcast_dynamic-update-slice_fusion.2 = bf16[8,4,4096]{2,1,0:T(4,128)(2,1)S(1)} fusion(bf16[8,4,4096]{2,1,0:T(4,128)(2,1)S(1)} %get-tuple-element.144, s32[]{:T(128)} %get-tuple-element.141, bf16[4,36864]{1,0:T(4,128)(2,1)} %get-tuple-element.147, s32[]{:T(128)} %bitcast.83), kind=kLoop, calls=%fused_computation.27.clone.1 | loop fusion | bytes 65544 | tf_op jit(solution)/shard_map/vmap()/gather
  46.0 1.4 %bitcast_dynamic-update-slice_fusion.2 = bf16[8,4,4096]{2,1,0:T(4,128)(2,1)S(1)} fusion(bf16[8,4,4096]{2,1,0:T(4,128)(2,1)S(1)} %get-tuple-element.144, s32[]{:T(128)} %get-tuple-element.141, bf16[4,36864]{1,0:T(4,128)(2,1)} %get-tuple-element.147, s32[]{:T(128)} %bitcast.83), kind=kLoop, calls=%fused_computation.27.clone.1 | loop fusion | bytes 65544 | tf_op jit(solution)/shard_map/vmap()/gather
  48.0 1.4 %bitcast_dynamic-update-slice_fusion.2 = bf16[8,4,4096]{2,1,0:T(4,128)(2,1)S(1)} fusion(bf16[8,4,4096]{2,1,0:T(4,128)(2,1)S(1)} %get-tuple-element.144, s32[]{:T(128)} %get-tuple-element.141, bf16[4,36864]{1,0:T(4,128)(2,1)} %get-tuple-element.147, s32[]{:T(128)} %bitcast.83), kind=kLoop, calls=%fused_computation.27.clone.1 | loop fusion | bytes 65544 | tf_op jit(solution)/shard_map/vmap()/gather
  50.0 1.4 %bitcast_dynamic-update-slice_fusion.2 = bf16[8,4,4096]{2,1,0:T(4,128)(2,1)S(1)} fusion(bf16[8,4,4096]{2,1,0:T(4,128)(2,1)S(1)} %get-tuple-element.144, s32[]{:T(128)} %get-tuple-element.141, bf16[4,36864]{1,0:T(4,128)(2,1)} %get-tuple-element.147, s32[]{:T(128)} %bitcast.83), kind=kLoop, calls=%fused_computation.27.clone.1 | loop fusion | bytes 65544 | tf_op jit(solution)/shard_map/vmap()/gather
  51.5 4.4 %multiply_reduce_fusion = (f32[32]{0:T(128)S(1)}, f32[32,1024]{1,0:T(8,128)S(1)}) fusion(bf16[4096,512]{1,0:T(8,128)(2,1)} %get-tuple-element.78, bf16[4096,512]{1,0:T(8,128)(2,1)} %get-tuple-element.79, bf16[8,4,4096]{2,1,0:T(4,128)(2,1)S(1)} %get-tuple-element.40), kind=kOutput, calls=%fused_computation.59 | convolution fusion | flops 285278176 | bytes 8781952 | tf_op jit(solution)/shard_map/dot_general | solution.py:32
  57.1 1.1 cosine_convert_fusion.1
  58.2 15.7 %all_gather.3 = bf16[16,8,1024]{2,1,0:T(8,128)(2,1)S(1)} all-gather(bf16[4,8,1024]{2,1,0:T(8,128)(2,1)S(1)} %fusion.39), channel_id=1, replica_groups=mesh['group'=2,'src'=4,'rcv'=4] {'src'}, dimensions={0}, use_global_device_ids=true | all-gather | bytes 327680 | tf_op jit(solution)/shard_map/all_gather | solution.py:71
  74.0 1.6 %copy.22 = bf16[16,8,1024]{0,1,2:T(8,128)(2,1)S(1)} copy(bf16[16,8,1024]{2,1,0:T(8,128)(2,1)S(1)} %all_gather.3) | data formatting | bytes 524288 | tf_op jit(solution)/shard_map/while | solution.py:57
  75.7 0.7 pad_maximum_fusion
  76.4 3.0 %collective-permute-done.1 = bf16[4,8,1024]{2,1,0:T(8,128)(2,1)S(1)} collective-permute-done((bf16[4,8,1024]{2,1,0:T(8,128)(2,1)S(1)}, bf16[4,8,1024]{2,1,0:T(8,128)(2,1)S(1)}, u32[]{:S(2)}, u32[]{:S(2)}) %collective-permute-start.1) | collective-permute-done | bytes 65568 | tf_op jit(solution)/shard_map/ppermute | solution.py:67
  80.0 3.1 %collective-permute-done.2 = bf16[4,8,1024]{2,1,0:T(8,128)(2,1)S(1)} collective-permute-done((bf16[4,8,1024]{2,1,0:T(8,128)(2,1)S(1)}, bf16[4,8,1024]{2,1,0:T(8,128)(2,1)S(1)}, u32[]{:S(2)}, u32[]{:S(2)}) %collective-permute-start.2) | collective-permute-done | bytes 65568 | tf_op jit(solution)/shard_map/ppermute | solution.py:67
  83.3 0.7 constant_dynamic-slice_fusion.2
  84.1 41.1 %while.11 = (s32[]{:T(128)}, bf16[4,4,16,128]{3,1,0,2:T(4,128)(2,1)}, bf16[4,4,8,1024]{3,2,1,0:T(8,128)(2,1)}, bf16[16,8,1024]{0,1,2:T(8,128)(2,1)S(1)}, bf16[1024,128]{1,0:T(8,128)(2,1)}, /*index=5*/s32[]{:T(128)}) while((s32[]{:T(128)}, bf16[4,4,16,128]{3,1,0,2:T(4,128)(2,1)}, bf16[4,4,8,1024]{3,2,1,0:T(8,128)(2,1)}, ...), condition=%wide.region_2.3_spmd, body=%wide.region_1.2_spmd.sunk | while | flops 19283968 | bytes 4768385 | solution.py:57
  84.1 0.8 constant_dynamic-slice_fusion.5
  85.6 0.7 fusion.97
  86.4 1.5 %fusion.99 = bf16[4,16,512]{1,0,2:T(4,128)(2,1)} fusion(f32[512,4,16]{2,1,0:T(4,128)S(1)} %fusion.97, bf16[1,4,8,1024]{2,1,3,0:T(4,128)(2,1)S(1)} %copy.40, bf16[16,8,512]{0,1,2:T(8,128)(2,1)S(1)} %fusion.98), kind=kOutput, calls=%fused_computation.6.clone.2 | convolution fusion | flops 589824 | bytes 393216 | tf_op jit(solution)/shard_map/while/body/eval_jaxpr/sgk,rgk->srk/dot_general | solution.py:45
  87.9 1.9 %copy.42 = bf16[4,16,512]{2,1,0:T(8,128)(2,1)} copy(bf16[4,16,512]{1,0,2:T(4,128)(2,1)} %fusion.99) | data formatting | bytes 131072 | tf_op jit(solution)/shard_map/while/body/eval_jaxpr/add | solution.py:47
  89.9 0.7 fusion.93
  90.7 1.5 %fusion.95 = bf16[4,16,512]{1,0,2:T(4,128)(2,1)} fusion(f32[512,4,16]{2,1,0:T(4,128)S(1)} %fusion.93, bf16[1,4,8,1024]{2,1,3,0:T(4,128)(2,1)S(1)} %copy.40, bf16[16,8,512]{0,1,2:T(8,128)(2,1)S(1)} %fusion.94), kind=kOutput, calls=%fused_computation.5.clone.2 | convolution fusion | flops 589824 | bytes 393216 | tf_op jit(solution)/shard_map/while/body/eval_jaxpr/sgk,rgk->srk/dot_general | solution.py:45
  92.2 1.3 copy.41
  94.3 0.8 constant_dynamic-slice_fusion.5
  95.9 0.7 fusion.97
  96.7 1.5 %fusion.99 = bf16[4,16,512]{1,0,2:T(4,128)(2,1)} fusion(f32[512,4,16]{2,1,0:T(4,128)S(1)} %fusion.97, bf16[1,4,8,1024]{2,1,3,0:T(4,128)(2,1)S(1)} %copy.40, bf16[16,8,512]{0,1,2:T(8,128)(2,1)S(1)} %fusion.98), kind=kOutput, calls=%fused_computation.6.clone.2 | convolution fusion | flops 589824 | bytes 393216 | tf_op jit(solution)/shard_map/while/body/eval_jaxpr/sgk,rgk->srk/dot_general | solution.py:45
  98.2 1.9 %copy.42 = bf16[4,16,512]{2,1,0:T(8,128)(2,1)} copy(bf16[4,16,512]{1,0,2:T(4,128)(2,1)} %fusion.99) | data formatting | bytes 131072 | tf_op jit(solution)/shard_map/while/body/eval_jaxpr/add | solution.py:47
  100.2 0.7 fusion.93
  101.0 1.5 %fusion.95 = bf16[4,16,512]{1,0,2:T(4,128)(2,1)} fusion(f32[512,4,16]{2,1,0:T(4,128)S(1)} %fusion.93, bf16[1,4,8,1024]{2,1,3,0:T(4,128)(2,1)S(1)} %copy.40, bf16[16,8,512]{0,1,2:T(8,128)(2,1)S(1)} %fusion.94), kind=kOutput, calls=%fused_computation.5.clone.2 | convolution fusion | flops 589824 | bytes 393216 | tf_op jit(solution)/shard_map/while/body/eval_jaxpr/sgk,rgk->srk/dot_general | solution.py:45
  102.5 1.3 copy.41
  104.6 0.8 constant_dynamic-slice_fusion.5
  106.2 0.7 fusion.97
  107.0 1.5 %fusion.99 = bf16[4,16,512]{1,0,2:T(4,128)(2,1)} fusion(f32[512,4,16]{2,1,0:T(4,128)S(1)} %fusion.97, bf16[1,4,8,1024]{2,1,3,0:T(4,128)(2,1)S(1)} %copy.40, bf16[16,8,512]{0,1,2:T(8,128)(2,1)S(1)} %fusion.98), kind=kOutput, calls=%fused_computation.6.clone.2 | convolution fusion | flops 589824 | bytes 393216 | tf_op jit(solution)/shard_map/while/body/eval_jaxpr/sgk,rgk->srk/dot_general | solution.py:45
  108.5 1.9 %copy.42 = bf16[4,16,512]{2,1,0:T(8,128)(2,1)} copy(bf16[4,16,512]{1,0,2:T(4,128)(2,1)} %fusion.99) | data formatting | bytes 131072 | tf_op jit(solution)/shard_map/while/body/eval_jaxpr/add | solution.py:47
  110.5 0.7 fusion.93
  111.3 1.5 %fusion.95 = bf16[4,16,512]{1,0,2:T(4,128)(2,1)} fusion(f32[512,4,16]{2,1,0:T(4,128)S(1)} %fusion.93, bf16[1,4,8,1024]{2,1,3,0:T(4,128)(2,1)S(1)} %copy.40, bf16[16,8,512]{0,1,2:T(8,128)(2,1)S(1)} %fusion.94), kind=kOutput, calls=%fused_computation.5.clone.2 | convolution fusion | flops 589824 | bytes 393216 | tf_op jit(solution)/shard_map/while/body/eval_jaxpr/sgk,rgk->srk/dot_general | solution.py:45
  112.8 1.3 copy.41
  114.9 0.8 constant_dynamic-slice_fusion.5
  116.5 0.7 fusion.97
  117.3 1.5 %fusion.99 = bf16[4,16,512]{1,0,2:T(4,128)(2,1)} fusion(f32[512,4,16]{2,1,0:T(4,128)S(1)} %fusion.97, bf16[1,4,8,1024]{2,1,3,0:T(4,128)(2,1)S(1)} %copy.40, bf16[16,8,512]{0,1,2:T(8,128)(2,1)S(1)} %fusion.98), kind=kOutput, calls=%fused_computation.6.clone.2 | convolution fusion | flops 589824 | bytes 393216 | tf_op jit(solution)/shard_map/while/body/eval_jaxpr/sgk,rgk->srk/dot_general | solution.py:45
  118.8 1.9 %copy.42 = bf16[4,16,512]{2,1,0:T(8,128)(2,1)} copy(bf16[4,16,512]{1,0,2:T(4,128)(2,1)} %fusion.99) | data formatting | bytes 131072 | tf_op jit(solution)/shard_map/while/body/eval_jaxpr/add | solution.py:47
  120.8 0.7 fusion.93
  121.6 1.5 %fusion.95 = bf16[4,16,512]{1,0,2:T(4,128)(2,1)} fusion(f32[512,4,16]{2,1,0:T(4,128)S(1)} %fusion.93, bf16[1,4,8,1024]{2,1,3,0:T(4,128)(2,1)S(1)} %copy.40, bf16[16,8,512]{0,1,2:T(8,128)(2,1)S(1)} %fusion.94), kind=kOutput, calls=%fused_computation.5.clone.2 | convolution fusion | flops 589824 | bytes 393216 | tf_op jit(solution)/shard_map/while/body/eval_jaxpr/sgk,rgk->srk/dot_general | solution.py:45
  123.1 1.3 copy.41
  125.2 1.5 %gather_fusion = bf16[16,16,128]{2,1,0:T(8,128)(2,1)S(1)} fusion(bf16[16,16,128]{2,0,1:T(8,128)(2,1)} %bitcast.84, s32[1024]{0:T(1024)} %pad_clamp_fusion), kind=kCustom, calls=%fused_computation | custom fusion | bytes 131136 | tf_op jit(solution)/shard_map/jit(_take)/gather | solution.py:72
  (90 shorter events, 14.6 us)
Async XLA Ops:
  0.0 35.1 %copy-start.3 = (s32[8]{0:T(128)S(1)}, s32[8]{0:T(128)}, u32[]{:S(2)}) copy-start(s32[8]{0:T(128)} %param.6) | copy-start | bytes 100
  51.5 5.1 %copy-start.4 = (s32[1,16]{1,0:T(1,128)S(1)}, s32[1,16]{1,0:T(1,128)}, u32[]{:S(2)}) copy-start(s32[1,16]{1,0:T(1,128)} %param.7) | copy-start | bytes 196
  56.0 19.6 %collective-permute-start = (bf16[4,8,1024]{2,1,0:T(8,128)(2,1)S(1)}, bf16[4,8,1024]{2,1,0:T(8,128)(2,1)S(1)}, u32[]{:S(2)}, u32[]{:S(2)}) collective-permute-start(bf16[4,8,1024]{2,1,0:T(8,128)(2,1)S(1)} %fusion.39), channel_id=1, source_target_pairs={{0,1},{1,2},{2,3},{3,0},{4,5},{5,6},{6,7},{7,4},{8,9},{9,10},{10,1... | collective-permute-start | bytes 196616 | tf_op jit(solution)/shard_map/ppermute | solution.py:67
  75.7 3.7 %collective-permute-start.1 = (bf16[4,8,1024]{2,1,0:T(8,128)(2,1)S(1)}, bf16[4,8,1024]{2,1,0:T(8,128)(2,1)S(1)}, u32[]{:S(2)}, u32[]{:S(2)}) collective-permute-start(bf16[4,8,1024]{2,1,0:T(8,128)(2,1)S(1)} %collective-permute-done), channel_id=1, source_target_pairs={{0,1},{1,2},{2,3},{3,0},{4,5},{5,6},{6,7},{7,4},{8,9},{9,10},{10,1... | collective-permute-start | bytes 196616 | tf_op jit(solution)/shard_map/ppermute | solution.py:67
  79.4 3.7 %collective-permute-start.2 = (bf16[4,8,1024]{2,1,0:T(8,128)(2,1)S(1)}, bf16[4,8,1024]{2,1,0:T(8,128)(2,1)S(1)}, u32[]{:S(2)}, u32[]{:S(2)}) collective-permute-start(bf16[4,8,1024]{2,1,0:T(8,128)(2,1)S(1)} %collective-permute-done.1), channel_id=1, source_target_pairs={{0,1},{1,2},{2,3},{3,0},{4,5},{5,6},{6,7},{7,4},{8,9},{9,10},{10,1... | collective-permute-start | bytes 196616 | tf_op jit(solution)/shard_map/ppermute | solution.py:67
  84.1 42.7 %copy-start.2 = (pred[16]{0:T(512)(128)(4,1)S(1)}, pred[16]{0:T(512)(128)(4,1)}, u32[]{:S(2)}) copy-start(pred[16]{0:T(512)(128)(4,1)} %compare_and_fusion) | copy-start | bytes 52
  90.7 2.8 %copy-start = (bf16[1024,128]{1,0:T(8,128)(2,1)S(1)}, bf16[1024,128]{1,0:T(8,128)(2,1)}, u32[]{:S(2)}) copy-start(bf16[1024,128]{1,0:T(8,128)(2,1)} %get-tuple-element.167) | copy-start | bytes 786436 | tf_op jit(solution)/shard_map/while
  90.7 2.8 %copy-start.1 = (bf16[4,16,512]{2,1,0:T(8,128)(2,1)S(1)}, bf16[4,16,512]{2,1,0:T(8,128)(2,1)}, u32[]{:S(2)}) copy-start(bf16[4,16,512]{2,1,0:T(8,128)(2,1)} %copy.42) | copy-start | bytes 196612 | tf_op jit(solution)/shard_map/while
  101.0 2.8 %copy-start = (bf16[1024,128]{1,0:T(8,128)(2,1)S(1)}, bf16[1024,128]{1,0:T(8,128)(2,1)}, u32[]{:S(2)}) copy-start(bf16[1024,128]{1,0:T(8,128)(2,1)} %get-tuple-element.167) | copy-start | bytes 786436 | tf_op jit(solution)/shard_map/while
  101.0 2.8 %copy-start.1 = (bf16[4,16,512]{2,1,0:T(8,128)(2,1)S(1)}, bf16[4,16,512]{2,1,0:T(8,128)(2,1)}, u32[]{:S(2)}) copy-start(bf16[4,16,512]{2,1,0:T(8,128)(2,1)} %copy.42) | copy-start | bytes 196612 | tf_op jit(solution)/shard_map/while
  111.3 2.8 %copy-start = (bf16[1024,128]{1,0:T(8,128)(2,1)S(1)}, bf16[1024,128]{1,0:T(8,128)(2,1)}, u32[]{:S(2)}) copy-start(bf16[1024,128]{1,0:T(8,128)(2,1)} %get-tuple-element.167) | copy-start | bytes 786436 | tf_op jit(solution)/shard_map/while
  111.3 2.8 %copy-start.1 = (bf16[4,16,512]{2,1,0:T(8,128)(2,1)S(1)}, bf16[4,16,512]{2,1,0:T(8,128)(2,1)}, u32[]{:S(2)}) copy-start(bf16[4,16,512]{2,1,0:T(8,128)(2,1)} %copy.42) | copy-start | bytes 196612 | tf_op jit(solution)/shard_map/while
  121.5 2.8 %copy-start = (bf16[1024,128]{1,0:T(8,128)(2,1)S(1)}, bf16[1024,128]{1,0:T(8,128)(2,1)}, u32[]{:S(2)}) copy-start(bf16[1024,128]{1,0:T(8,128)(2,1)} %get-tuple-element.167) | copy-start | bytes 786436 | tf_op jit(solution)/shard_map/while
  121.6 2.8 %copy-start.1 = (bf16[4,16,512]{2,1,0:T(8,128)(2,1)S(1)}, bf16[4,16,512]{2,1,0:T(8,128)(2,1)}, u32[]{:S(2)}) copy-start(bf16[4,16,512]{2,1,0:T(8,128)(2,1)} %copy.42) | copy-start | bytes 196612 | tf_op jit(solution)/shard_map/while
